TPU v7x, 32 devices: a whole 2x2x4 slice. The times are simulated.
32 devices in a mesh: replica: 8 (over y, x, core), group: 4 (over z).
Axes of the slice: x: 2, y: 2, z: 4, core: 2. Of those that a mesh axis runs over, the one named last changes fastest.
Arguments:
- inputs: bfloat16 [8, 512, 2048], P('replica', 'group'), may hold values from -6 to 6
- seq_lengths: int32 [8], P('replica'), may hold values from 128 to 512, as said below
- bucket_ids: int32 [1023], replicated, may hold values from 0 to 31, as said below
- norm1_gain: bfloat16 [2048], P('group'), may hold values from 0.25 to 1.75
- w_query: bfloat16 [2048, 2048], P(None, 'group'), may hold values from -0.0625 to 0.0625
- w_key: bfloat16 [2048, 2048], P(None, 'group'), may hold values from -0.0625 to 0.0625
- w_value: bfloat16 [2048, 2048], P(None, 'group'), may hold values from -0.125 to 0.125
- w_attn_out: bfloat16 [2048, 2048], P('group'), may hold values from -0.5 to 0.5
- bias_table: bfloat16 [32, 32], P(None, 'group'), may hold values from -4 to 4
- norm2_gain: bfloat16 [2048], P('group'), may hold values from 0.25 to 1.75
- w_gate: bfloat16 [2048, 5120], P(None, 'group'), may hold values from -0.125 to 0.125
- w_up: bfloat16 [2048, 5120], P(None, 'group'), may hold values from -0.125 to 0.125
- w_ffn_out: bfloat16 [5120, 2048], P('group'), may hold values from -0.078125 to 0.078125
- cotangent: bfloat16 [8, 512, 2048], P('replica', 'group'), may hold values from -6 to 6
Outputs:
- result: bfloat16 [8, 512, 2048], P('replica', 'group')
- input_grad: bfloat16 [8, 512, 2048], P('replica', 'group')
- norm1_gain_grad: float32 [2048], P('group')
- query_grad: float32 [2048, 2048], P(None, 'group')
- key_grad: float32 [2048, 2048], P(None, 'group')
- value_grad: float32 [2048, 2048], P(None, 'group')
- attn_out_grad: float32 [2048, 2048], P('group')
- bias_table_grad: float32 [32, 32], P(None, 'group')
- norm2_gain_grad: float32 [2048], P('group')
- gate_grad: float32 [2048, 5120], P(None, 'group')
- up_grad: float32 [2048, 5120], P(None, 'group')
- ffn_out_grad: float32 [5120, 2048], P('group')
Inputs may be any that keep to these rules, and one draw needn't show every extreme that they name: `seq_lengths`: one sequence has exactly 512 valid positions and another exactly 128. `bucket_ids`: entry 511 + o is the bucket of the offset o = key position - query position; every bucket occurs.
All inputs are finite; a program needn't handle non-finite values.
Results may differ from a plain program's by a relative error of at most 0.02.
Values may be sent and summed in bfloat16 or wider, within the bound.
A program may use at most 448 MiB of HBM per device.

v0:
```python
import jax
import jax.numpy as jnp
from jax import lax
from jax.sharding import PartitionSpec as P

epsilon = 1e-06
negative = -1000000000.0
head_block = 8
highest = lax.Precision.HIGHEST


def rms_scale(values, gain):
    return values * lax.rsqrt(jnp.mean(values * values, axis=-1, keepdims=True) + epsilon) * gain


def gated_gelu(gate_pre, up_pre):
    return jax.nn.gelu(gate_pre, approximate=True) * up_pre


def inner_rows(left, right):
    return lax.dot_general(
        left, right, (((0,), (0,)), ((), ())), preferred_element_type=jnp.float32
    )


def inner_columns(left, right):
    return lax.dot_general(
        left, right, (((1,), (1,)), ((), ())), preferred_element_type=jnp.float32
    )


def split_heads(matrix, groups, block_size):
    return matrix.reshape(matrix.shape[0], groups, block_size, -1).transpose(1, 0, 2, 3)


def merge_heads(blocks):
    return blocks.transpose(1, 0, 2, 3).reshape(blocks.shape[1], -1)


def spread_offsets(vector, row_count, col_count):
    span_width = row_count + col_count + 1
    block_heads = vector.shape[0]
    tiled_rows = jnp.broadcast_to(vector[:, None, :], (block_heads, row_count, span_width))
    flattened = tiled_rows.reshape(block_heads, row_count * span_width)[
        :, : row_count * (span_width - 1)
    ]
    return flattened.reshape(block_heads, row_count, span_width - 1)[:, :, row_count:]


def fold_offsets(matrix):
    block_heads, row_count, col_count = matrix.shape
    padded = jnp.pad(matrix, ((0, 0), (0, 0), (row_count, 0)))
    flattened = jnp.pad(
        padded.reshape(block_heads, row_count * (row_count + col_count)), ((0, 0), (0, row_count))
    )
    sums_all = flattened.reshape(block_heads, row_count, row_count + col_count + 1).sum(axis=1)
    return sums_all[:, 1 : row_count + col_count]


def offset_table(table_part, one_hot, groups, block_size):
    per_offset = jnp.dot(one_hot, table_part.astype(jnp.float32), precision=highest)
    return jnp.pad(per_offset.T, ((0, 0), (1, 1))).reshape(groups, block_size, -1)


def attention_forward(query_low, key_all, value_all, offsets, key_valid, groups, block_size):
    row_count = query_low.shape[0]
    keys_total = key_all.shape[0]

    def attend_block(operands):
        query_blk, key_blk, value_blk, offset_blk = operands
        scores = jnp.einsum("qhd,khd->hqk", query_blk, key_blk, preferred_element_type=jnp.float32)
        scores = jnp.where(
            key_valid, scores + spread_offsets(offset_blk, row_count, keys_total), negative
        )
        top_score = jnp.max(scores, axis=-1, keepdims=True)
        weights_exp = jnp.exp(scores - top_score)
        total_exp = jnp.sum(weights_exp, axis=-1, keepdims=True)
        probs_low = (weights_exp / total_exp).astype(jnp.bfloat16)
        attended_blk = jnp.einsum(
            "hqk,khd->qhd", probs_low, value_blk, preferred_element_type=jnp.float32
        )
        return (attended_blk, top_score[..., 0] + jnp.log(total_exp[..., 0]))

    operands = (
        split_heads(query_low, groups, block_size),
        split_heads(key_all, groups, block_size),
        split_heads(value_all, groups, block_size),
        offsets,
    )
    attended, log_totals = lax.map(attend_block, operands)
    return (merge_heads(attended).astype(jnp.bfloat16), log_totals)


def attention_backward(
    query_low, key_all, value_all, offsets, key_valid, grad_attended, log_totals, groups, block_size
):
    row_count = query_low.shape[0]
    keys_total = key_all.shape[0]

    def attend_back(operands):
        query_blk, key_blk, value_blk, offset_blk, grad_blk, log_blk = operands
        scores = jnp.einsum("qhd,khd->hqk", query_blk, key_blk, preferred_element_type=jnp.float32)
        scores = jnp.where(
            key_valid, scores + spread_offsets(offset_blk, row_count, keys_total), negative
        )
        probs = jnp.exp(scores - log_blk[..., None])
        grad_probs = jnp.einsum(
            "qhd,khd->hqk", grad_blk, value_blk, preferred_element_type=jnp.float32
        )
        inner_sum = jnp.sum(probs * grad_probs, axis=-1, keepdims=True)
        grad_scores = (probs * (grad_probs - inner_sum)).astype(jnp.bfloat16)
        probs_low = probs.astype(jnp.bfloat16)
        grad_query = jnp.einsum(
            "hqk,khd->qhd", grad_scores, key_blk, preferred_element_type=jnp.float32
        )
        grad_key = jnp.einsum(
            "hqk,qhd->khd", grad_scores, query_blk, preferred_element_type=jnp.float32
        )
        grad_value = jnp.einsum(
            "hqk,qhd->khd", probs_low, grad_blk, preferred_element_type=jnp.float32
        )
        return (grad_query, grad_key, grad_value, fold_offsets(grad_scores.astype(jnp.float32)))

    operands = (
        split_heads(query_low, groups, block_size),
        split_heads(key_all, groups, block_size),
        split_heads(value_all, groups, block_size),
        offsets,
        split_heads(grad_attended, groups, block_size),
        log_totals,
    )
    grad_query_blk, grad_key_blk, grad_value_blk, offset_sums = lax.map(attend_back, operands)
    return (
        merge_heads(grad_query_blk),
        merge_heads(grad_key_blk),
        merge_heads(grad_value_blk),
        offset_sums,
    )


def local(
    inputs,
    seq_lengths,
    bucket_ids,
    norm1_gain,
    w_query,
    w_key,
    w_value,
    w_attn_out,
    bias_table,
    norm2_gain,
    w_gate,
    w_up,
    w_ffn_out,
    cotangent,
):
    hidden_in = inputs[0].astype(jnp.float32)
    row_count = hidden_in.shape[0]
    keys_total = row_count * lax.axis_size("group")
    query_start = lax.axis_index("group") * row_count
    length = seq_lengths[0]
    buckets = bias_table.shape[0]
    key_valid = (jnp.arange(keys_total) < length)[None, None, :]
    row_valid = query_start + jnp.arange(row_count) < length
    gain_one, gain_two, query_full, key_full, value_full, attn_full, table_full = (
        lax.all_gather(norm1_gain, "group", axis=0, tiled=True),
        lax.all_gather(norm2_gain, "group", axis=0, tiled=True),
        lax.all_gather(w_query, "group", axis=1, tiled=True),
        lax.all_gather(w_key, "group", axis=1, tiled=True),
        lax.all_gather(w_value, "group", axis=1, tiled=True),
        lax.all_gather(w_attn_out, "group", axis=0, tiled=True),
        lax.all_gather(bias_table, "group", axis=1, tiled=True),
    )
    gain_first = gain_one.astype(jnp.float32)
    gain_second = gain_two.astype(jnp.float32)
    head_count = table_full.shape[1]
    groups = head_count // head_block
    normed_one = rms_scale(hidden_in, gain_first).astype(jnp.bfloat16)
    query_low = jnp.dot(normed_one, query_full, preferred_element_type=jnp.float32).astype(
        jnp.bfloat16
    )
    key_low = jnp.dot(normed_one, key_full, preferred_element_type=jnp.float32).astype(jnp.bfloat16)
    value_low = jnp.dot(normed_one, value_full, preferred_element_type=jnp.float32).astype(
        jnp.bfloat16
    )
    key_all, value_all = (
        lax.all_gather(key_low, "group", axis=0, tiled=True),
        lax.all_gather(value_low, "group", axis=0, tiled=True),
    )
    window = lax.dynamic_slice_in_dim(
        bucket_ids, keys_total - row_count - query_start, row_count + keys_total - 1
    )
    one_hot = (window[:, None] == jnp.arange(buckets)[None, :]).astype(jnp.float32)
    offsets = offset_table(table_full, one_hot, groups, head_block)
    attended_low, log_totals = attention_forward(
        query_low, key_all, value_all, offsets, key_valid, groups, head_block
    )
    middle = hidden_in + jnp.dot(attended_low, attn_full, preferred_element_type=jnp.float32)
    normed_two = rms_scale(middle, gain_second).astype(jnp.bfloat16)
    grad_out = cotangent[0].astype(jnp.float32) * row_valid[:, None].astype(jnp.float32)
    grad_low = grad_out.astype(jnp.bfloat16)
    gate_full, up_full, ffn_full = (
        lax.all_gather(w_gate, "group", axis=1, tiled=True),
        lax.all_gather(w_up, "group", axis=1, tiled=True),
        lax.all_gather(w_ffn_out, "group", axis=0, tiled=True),
    )
    gate_pre = jnp.dot(normed_two, gate_full, preferred_element_type=jnp.float32)
    up_pre = jnp.dot(normed_two, up_full, preferred_element_type=jnp.float32)
    hidden_low = gated_gelu(gate_pre, up_pre).astype(jnp.bfloat16)
    branch_ffn = jnp.dot(hidden_low, ffn_full, preferred_element_type=jnp.float32)
    result = (middle + branch_ffn).astype(jnp.bfloat16)
    gate_back, up_back, ffn_back = (
        lax.all_gather(w_gate, "group", axis=1, tiled=True),
        lax.all_gather(w_up, "group", axis=1, tiled=True),
        lax.all_gather(w_ffn_out, "group", axis=0, tiled=True),
    )
    grad_hidden = inner_columns(grad_low, ffn_back)
    _, pull_gelu = jax.vjp(gated_gelu, gate_pre, up_pre)
    grad_gate, grad_up = pull_gelu(grad_hidden)
    grad_gate = grad_gate.astype(jnp.bfloat16)
    grad_up = grad_up.astype(jnp.bfloat16)
    grad_normed = inner_columns(grad_gate, gate_back) + inner_columns(grad_up, up_back)
    gate_grad, up_grad, ffn_out_grad = (
        lax.psum_scatter(
            inner_rows(normed_two, grad_gate).astype(jnp.bfloat16),
            "group",
            scatter_dimension=1,
            tiled=True,
        ).astype(jnp.float32),
        lax.psum_scatter(
            inner_rows(normed_two, grad_up).astype(jnp.bfloat16),
            "group",
            scatter_dimension=1,
            tiled=True,
        ).astype(jnp.float32),
        lax.psum_scatter(
            inner_rows(hidden_low, grad_low).astype(jnp.bfloat16),
            "group",
            scatter_dimension=0,
            tiled=True,
        ).astype(jnp.float32),
    )
    _, pull_two = jax.vjp(rms_scale, middle, gain_second)
    grad_mid_norm, gain_two_grad = pull_two(grad_normed)
    grad_middle = grad_out + grad_mid_norm
    grad_branch = grad_middle.astype(jnp.bfloat16)
    query_back, key_back, value_back, attn_back, table_back = (
        lax.all_gather(w_query, "group", axis=1, tiled=True),
        lax.all_gather(w_key, "group", axis=1, tiled=True),
        lax.all_gather(w_value, "group", axis=1, tiled=True),
        lax.all_gather(w_attn_out, "group", axis=0, tiled=True),
        lax.all_gather(bias_table, "group", axis=1, tiled=True),
    )
    attn_out_grad = inner_rows(attended_low, grad_branch)
    grad_attended = inner_columns(grad_branch, attn_back).astype(jnp.bfloat16)
    offset_bwd = offset_table(table_back, one_hot, groups, head_block)
    grad_query, grad_key, grad_value, offset_sums = attention_backward(
        query_low,
        key_all,
        value_all,
        offset_bwd,
        key_valid,
        grad_attended,
        log_totals,
        groups,
        head_block,
    )
    key_sum, value_sum = (
        lax.psum_scatter(
            grad_key.astype(jnp.bfloat16), "group", scatter_dimension=0, tiled=True
        ).astype(jnp.float32),
        lax.psum_scatter(
            grad_value.astype(jnp.bfloat16), "group", scatter_dimension=0, tiled=True
        ).astype(jnp.float32),
    )
    grad_query_low = grad_query.astype(jnp.bfloat16)
    grad_key_low = key_sum.astype(jnp.bfloat16)
    grad_value_low = value_sum.astype(jnp.bfloat16)
    table_grad = jnp.dot(offset_sums.reshape(head_count, -1), one_hot, precision=highest).T
    query_grad = inner_rows(normed_one, grad_query_low)
    key_grad = inner_rows(normed_one, grad_key_low)
    value_grad = inner_rows(normed_one, grad_value_low)
    grad_normed_one = (
        inner_columns(grad_query_low, query_back)
        + inner_columns(grad_key_low, key_back)
        + inner_columns(grad_value_low, value_back)
    )
    _, pull_one = jax.vjp(rms_scale, hidden_in, gain_first)
    grad_in_norm, gain_one_grad = pull_one(grad_normed_one)
    input_grad = (grad_middle + grad_in_norm).astype(jnp.bfloat16)
    gain_one_part, gain_two_part, query_part, key_part, value_part, attn_part, table_part = (
        lax.psum_scatter(
            gain_one_grad.astype(jnp.bfloat16), "group", scatter_dimension=0, tiled=True
        ).astype(jnp.float32),
        lax.psum_scatter(
            gain_two_grad.astype(jnp.bfloat16), "group", scatter_dimension=0, tiled=True
        ).astype(jnp.float32),
        lax.psum_scatter(
            query_grad.astype(jnp.bfloat16), "group", scatter_dimension=1, tiled=True
        ).astype(jnp.float32),
        lax.psum_scatter(
            key_grad.astype(jnp.bfloat16), "group", scatter_dimension=1, tiled=True
        ).astype(jnp.float32),
        lax.psum_scatter(
            value_grad.astype(jnp.bfloat16), "group", scatter_dimension=1, tiled=True
        ).astype(jnp.float32),
        lax.psum_scatter(
            attn_out_grad.astype(jnp.bfloat16), "group", scatter_dimension=0, tiled=True
        ).astype(jnp.float32),
        lax.psum_scatter(
            table_grad.astype(jnp.bfloat16), "group", scatter_dimension=1, tiled=True
        ).astype(jnp.float32),
    )
    summed = (
        lax.psum(gain_one_part.astype(jnp.bfloat16), "replica").astype(jnp.float32),
        lax.psum(query_part.astype(jnp.bfloat16), "replica").astype(jnp.float32),
        lax.psum(key_part.astype(jnp.bfloat16), "replica").astype(jnp.float32),
        lax.psum(value_part.astype(jnp.bfloat16), "replica").astype(jnp.float32),
        lax.psum(attn_part.astype(jnp.bfloat16), "replica").astype(jnp.float32),
        lax.psum(table_part.astype(jnp.bfloat16), "replica").astype(jnp.float32),
        lax.psum(gain_two_part.astype(jnp.bfloat16), "replica").astype(jnp.float32),
        lax.psum(gate_grad.astype(jnp.bfloat16), "replica").astype(jnp.float32),
        lax.psum(up_grad.astype(jnp.bfloat16), "replica").astype(jnp.float32),
        lax.psum(ffn_out_grad.astype(jnp.bfloat16), "replica").astype(jnp.float32),
    )
    return (
        result[None],
        input_grad[None],
        summed[0],
        summed[1],
        summed[2],
        summed[3],
        summed[4],
        summed[5],
        summed[6],
        summed[7],
        summed[8],
        summed[9],
    )


def solution(mesh):
    placed = (
        P("replica", "group", None),
        P("replica"),
        P(),
        P("group"),
        P(None, "group"),
        P(None, "group"),
        P(None, "group"),
        P("group", None),
        P(None, "group"),
        P("group"),
        P(None, "group"),
        P(None, "group"),
        P("group", None),
        P("replica", "group", None),
    )
    return jax.shard_map(
        local,
        mesh=mesh,
        in_specs=placed,
        out_specs=(
            P("replica", "group", None),
            P("replica", "group", None),
            P("group"),
            P(None, "group"),
            P(None, "group"),
            P(None, "group"),
            P("group", None),
            P(None, "group"),
            P("group"),
            P(None, "group"),
            P(None, "group"),
            P("group", None),
        ),
        check_vma=False,
    )
```

profile of v0, /device:TPU:0, one launch (start us, length us, event | category | flops | bytes accessed | tf_op | source)
XLA Modules:
  0.0 4007.4 jit_solution(15519130537218076561)
XLA Ops:
  23.3 138.7 %all-gather.12.cloned.1.call-done = bf16[2048,2048]{1,0:T(8,128)(2,1)} async-done(((bf16[2048,512]{1,0:T(8,128)(2,1)}), bf16[2048,2048]{1,0:T(8,128)(2,1)}) %all-gather.12.cloned.1.call-update) | async-done | bytes 8388624 | tf_op jit(solution)/shard_map/all_gather | solution.py:170
  167.5 143.9 %all-gather.18.cloned.1.call-done = bf16[2048,2048]{1,0:T(8,128)(2,1)} async-done(((bf16[2048,512]{1,0:T(8,128)(2,1)}), bf16[2048,2048]{1,0:T(8,128)(2,1)}) %all-gather.18.cloned.1.call-update) | async-done | bytes 8388624 | tf_op jit(solution)/shard_map/all_gather | solution.py:169
  319.9 15.4 all-gather.1
  350.1 110.9 %all-gather.16.cloned.1.call-done = bf16[2048,2048]{1,0:T(8,128)(2,1)} async-done(((bf16[2048,512]{1,0:T(8,128)(2,1)}), bf16[2048,2048]{1,0:T(8,128)(2,1)}) %all-gather.16.cloned.1.call-update) | async-done | bytes 8388624 | tf_op jit(solution)/shard_map/all_gather | solution.py:168
  466.8 40.4 %all-gather.14.cloned.1.call-done = bf16[512,2048]{1,0:T(8,128)(2,1)} async-done(((bf16[128,2048]{1,0:T(8,128)(2,1)}), bf16[512,2048]{1,0:T(8,128)(2,1)}) %all-gather.14.cloned.1.call-update) | async-done | bytes 2097168 | tf_op jit(solution)/shard_map/all_gather | solution.py:188
  511.1 42.8 %all-gather.20.cloned.1.call-done = bf16[512,2048]{1,0:T(8,128)(2,1)} async-done(((bf16[128,2048]{1,0:T(8,128)(2,1)}), bf16[512,2048]{1,0:T(8,128)(2,1)}) %all-gather.20.cloned.1.call-update) | async-done | bytes 2097168 | tf_op jit(solution)/shard_map/all_gather | solution.py:187
  558.7 46.0 %while.32 = (s32[]{:T(128)}, bf16[4,128,8,64]{1,3,2,0:T(8,128)(2,1)}, f32[4,8,128]{2,1,0:T(8,128)S(1)}, bf16[4,512,8,64]{1,3,2,0:T(8,128)(2,1)}, bf16[4,128,8,64...) while((s32[]{:T(128)}, ...), condition=%wide.region_4.5_spmd.clone, body=%wide.region_1.4_spmd.clone.sunk | while | flops 138411520 | bytes 35106080 | solution.py:90
  604.7 98.9 %all-gather.22.cloned.1.call-done = bf16[2048,2048]{1,0:T(8,128)(2,1)} async-done(((bf16[512,2048]{1,0:T(8,128)(2,1)}), bf16[2048,2048]{1,0:T(8,128)(2,1)}) %all-gather.22.cloned.1.call-update) | async-done | bytes 8388624 | tf_op jit(solution)/shard_map/all_gather | solution.py:171
  708.8 351.5 %all-gather.24.cloned.1.call-done = bf16[2048,5120]{1,0:T(8,128)(2,1)} async-done(((bf16[2048,1280]{1,0:T(8,128)(2,1)}), bf16[2048,5120]{1,0:T(8,128)(2,1)}) %all-gather.24.cloned.1.call-update) | async-done | bytes 20971536 | tf_op jit(solution)/shard_map/all_gather | solution.py:203
  1072.1 345.3 %all-gather.26.cloned.1.call-done = bf16[2048,5120]{1,0:T(8,128)(2,1)} async-done(((bf16[2048,1280]{1,0:T(8,128)(2,1)}), bf16[2048,5120]{1,0:T(8,128)(2,1)}) %all-gather.26.cloned.1.call-update) | async-done | bytes 20971536 | tf_op jit(solution)/shard_map/all_gather | solution.py:204
  1429.1 345.3 %all-gather.28.cloned.1.call-done = bf16[5120,2048]{1,0:T(8,128)(2,1)} async-done(((bf16[1280,2048]{1,0:T(8,128)(2,1)}), bf16[5120,2048]{1,0:T(8,128)(2,1)}) %all-gather.28.cloned.1.call-update) | async-done | bytes 20971536 | tf_op jit(solution)/shard_map/all_gather | solution.py:205
  1774.4 14.3 multiply_convert_fusion.1
  1822.0 106.5 %while.33 = (s32[]{:T(128)}, bf16[4,128,8,64]{1,3,2,0:T(8,128)(2,1)}, bf16[4,512,8,64]{1,3,2,0:T(8,128)(2,1)}, bf16[4,512,8,64]{1,3,2,0:T(8,128)(2,1)}, f32[4,8,...) while((s32[]{:T(128)}, ...), condition=%wide.region_10.11_spmd.clone, body=%wide.region_7.10_spmd.clone.sunk | while | flops 341570048 | bytes 102152648 | solution.py:132
  1949.1 26.1 reduce-scatter.28.cloned.1.call-done
  1982.1 39.2 reduce-scatter.30.cloned.1.call-done
  2063.4 104.6 %reduce-scatter.14.cloned.1.call-done = bf16[2048,512]{1,0:T(8,128)(2,1)} async-done(((bf16[2048,2048]{1,0:T(8,128)(2,1)}), bf16[2048,512]{1,0:T(8,128)(2,1)}) %reduce-scatter.14.cloned.1.call-update) | async-done | bytes 2097168 | tf_op jit(solution)/shard_map/reduce_scatter | solution.py:298
  2168.0 147.6 %reduce-scatter.20.cloned.1.call-done = bf16[512,2048]{1,0:T(8,128)(2,1)} async-done(((bf16[2048,2048]{1,0:T(8,128)(2,1)}), bf16[512,2048]{1,0:T(8,128)(2,1)}) %reduce-scatter.20.cloned.1.call-update) | async-done | bytes 2097168 | tf_op jit(solution)/shard_map/reduce_scatter | solution.py:307
  2315.6 148.0 %reduce-scatter.16.cloned.1.call-done = bf16[2048,512]{1,0:T(8,128)(2,1)} async-done(((bf16[2048,2048]{1,0:T(8,128)(2,1)}), bf16[2048,512]{1,0:T(8,128)(2,1)}) %reduce-scatter.16.cloned.1.call-update) | async-done | bytes 2097168 | tf_op jit(solution)/shard_map/reduce_scatter | solution.py:301
  2463.6 148.0 %reduce-scatter.18.cloned.1.call-done = bf16[2048,512]{1,0:T(8,128)(2,1)} async-done(((bf16[2048,2048]{1,0:T(8,128)(2,1)}), bf16[2048,512]{1,0:T(8,128)(2,1)}) %reduce-scatter.18.cloned.1.call-update) | async-done | bytes 2097168 | tf_op jit(solution)/shard_map/reduce_scatter | solution.py:304
  2611.6 350.2 %reduce-scatter.22.cloned.1.call-done = bf16[2048,1280]{1,0:T(8,128)(2,1)} async-done(((bf16[2048,5120]{1,0:T(8,128)(2,1)}), bf16[2048,1280]{1,0:T(8,128)(2,1)}) %reduce-scatter.22.cloned.1.call-update) | async-done | bytes 5242896 | tf_op jit(solution)/shard_map/reduce_scatter | solution.py:224
  2961.8 351.0 %reduce-scatter.24.cloned.1.call-done = bf16[2048,1280]{1,0:T(8,128)(2,1)} async-done(((bf16[2048,5120]{1,0:T(8,128)(2,1)}), bf16[2048,1280]{1,0:T(8,128)(2,1)}) %reduce-scatter.24.cloned.1.call-update) | async-done | bytes 5242896 | tf_op jit(solution)/shard_map/reduce_scatter | solution.py:230
  3312.8 350.9 %reduce-scatter.26.cloned.1.call-done = bf16[1280,2048]{1,0:T(8,128)(2,1)} async-done(((bf16[5120,2048]{1,0:T(8,128)(2,1)}), bf16[1280,2048]{1,0:T(8,128)(2,1)}) %reduce-scatter.26.cloned.1.call-update) | async-done | bytes 5242896 | tf_op jit(solution)/shard_map/reduce_scatter | solution.py:236
  3691.3 18.9 all-reduce.8
  3726.2 245.3 %all-reduce.11.cloned.1.call-done = (bf16[2048,512]{1,0:T(8,128)(2,1)}, bf16[2048,512]{1,0:T(8,128)(2,1)}, bf16[2048,512]{1,0:T(8,128)(2,1)}, bf16[512,2048]{1,0...) async-done(((bf16[2048,512]{1,0:T(8,128)(2,1)}, bf16[2048,512]{1,0:T(8,128)(2,1)}, bf16[2048,512]{1,0:T(8,128)(2,1)}, ...) | async-done | bytes 24117264 | tf_op jit(solution)/shard_map/psum | solution.py:316
  (384 shorter events, 411.9 us)
Async XLA Ops:
  7.2 154.8 %all-gather.12.cloned.1.call-start = ((), (), s32[]{:S(2)}) async-start(), calls=%async_computation.9 | async-start | bytes 10485760 | tf_op jit(solution)/shard_map/all_gather | solution.py:170
  7.9 303.5 %all-gather.18.cloned.1.call-start = ((), (), s32[]{:S(2)}) async-start(), calls=%async_computation.12 | async-start | bytes 10485760 | tf_op jit(solution)/shard_map/all_gather | solution.py:169
  8.7 452.4 %all-gather.16.cloned.1.call-start = ((), (), s32[]{:S(2)}) async-start(), calls=%async_computation.11 | async-start | bytes 10485760 | tf_op jit(solution)/shard_map/all_gather | solution.py:168
  9.4 497.8 %all-gather.14.cloned.1.call-start = ((), (), s32[]{:S(2)}) async-start(), calls=%async_computation.10 | async-start | bytes 2621440 | tf_op jit(solution)/shard_map/all_gather | solution.py:188
  23.1 438.0 %copy-start.16 = (f32[4,1,512]{2,1,0:T(1,128)}, f32[4,1,512]{2,1,0:T(1,128)S(1)}, u32[]{:S(2)}) copy-start(f32[4,1,512]{2,1,0:T(1,128)S(1)} %convert_element_type.283) | copy-start | bytes 24580
  23.3 437.8 %copy-start.30 = (f32[128]{0:T(128)}, f32[128]{0:T(128)S(1)}, u32[]{:S(2)}) copy-start(f32[128]{0:T(128)S(1)} %fusion.81) | copy-start | bytes 1540
  167.5 386.4 %all-gather.20.cloned.1.call-start = ((), (), s32[]{:S(2)}) async-start(), calls=%async_computation.13 | async-start | bytes 2621440 | tf_op jit(solution)/shard_map/all_gather | solution.py:187
  316.9 386.8 %all-gather.22.cloned.1.call-start = ((), (), s32[]{:S(2)}) async-start(), calls=%async_computation.14 | async-start | bytes 10485760 | tf_op jit(solution)/shard_map/all_gather | solution.py:171
  317.5 742.9 %all-gather.24.cloned.1.call-start = ((), (), s32[]{:S(2)}) async-start(), calls=%async_computation.15 | async-start | bytes 26214400 | tf_op jit(solution)/shard_map/all_gather | solution.py:203
  318.2 1099.1 %all-gather.26.cloned.1.call-start = ((), (), s32[]{:S(2)}) async-start(), calls=%async_computation.16 | async-start | bytes 26214400 | tf_op jit(solution)/shard_map/all_gather | solution.py:204
  319.0 1455.4 %all-gather.28.cloned.1.call-start = ((), (), s32[]{:S(2)}) async-start(), calls=%async_computation.17 | async-start | bytes 26214400 | tf_op jit(solution)/shard_map/all_gather | solution.py:205
  319.7 1655.4 %reduce-scatter.28.cloned.1.call-start = ((), (), s32[]{:S(2)}) async-start(), calls=%async_computation.25 | async-start | bytes 2621440
  708.6 1105.9 %copy-start.3 = (f32[128,2048]{1,0:T(8,128)}, f32[128,2048]{1,0:T(8,128)S(1)}, u32[]{:S(2)}) copy-start(f32[128,2048]{1,0:T(8,128)S(1)} %get-tuple-element.324) | copy-start | bytes 3145732
  708.8 708.6 %copy-start.7 = (bf16[128,2048]{1,0:T(8,128)(2,1)}, bf16[128,2048]{1,0:T(8,128)(2,1)S(1)}, u32[]{:S(2)}) copy-start(bf16[128,2048]{1,0:T(8,128)(2,1)S(1)} %multiply_convert_fusion.3) | copy-start | bytes 1572868
  1072.1 702.3 %copy-start.18 = (bf16[1,128,2048]{2,1,0:T(8,128)(2,1)S(1)}, bf16[1,128,2048]{2,1,0:T(8,128)(2,1)}, u32[]{:S(2)}) copy-start(bf16[1,128,2048]{2,1,0:T(8,128)(2,1)} %param.31) | copy-start | bytes 1572868
  1932.6 88.8 %reduce-scatter.30.cloned.1.call-start = ((), (), s32[]{:S(2)}) async-start(), calls=%async_computation.26 | async-start | bytes 2621440
  1935.1 232.9 %reduce-scatter.14.cloned.1.call-start = ((), (), s32[]{:S(2)}) async-start(), calls=%async_computation.18 | async-start | bytes 10485760 | tf_op jit(solution)/shard_map/reduce_scatter | solution.py:298
  1942.1 373.5 %reduce-scatter.20.cloned.1.call-start = ((), (), s32[]{:S(2)}) async-start(), calls=%async_computation.21 | async-start | bytes 10485760 | tf_op jit(solution)/shard_map/reduce_scatter | solution.py:307
  1949.0 514.6 %reduce-scatter.16.cloned.1.call-start = ((), (), s32[]{:S(2)}) async-start(), calls=%async_computation.19 | async-start | bytes 10485760 | tf_op jit(solution)/shard_map/reduce_scatter | solution.py:301
  1982.1 629.5 %reduce-scatter.18.cloned.1.call-start = ((), (), s32[]{:S(2)}) async-start(), calls=%async_computation.20 | async-start | bytes 10485760 | tf_op jit(solution)/shard_map/reduce_scatter | solution.py:304
  2028.3 933.5 %reduce-scatter.22.cloned.1.call-start = ((), (), s32[]{:S(2)}) async-start(), calls=%async_computation.22 | async-start | bytes 26214400 | tf_op jit(solution)/shard_map/reduce_scatter | solution.py:224
  2040.2 1272.6 %reduce-scatter.24.cloned.1.call-start = ((), (), s32[]{:S(2)}) async-start(), calls=%async_computation.23 | async-start | bytes 26214400 | tf_op jit(solution)/shard_map/reduce_scatter | solution.py:230
  2051.7 1612.0 %reduce-scatter.26.cloned.1.call-start = ((), (), s32[]{:S(2)}) async-start(), calls=%async_computation.24 | async-start | bytes 26214400 | tf_op jit(solution)/shard_map/reduce_scatter | solution.py:236
  2063.2 1908.4 %all-reduce.11.cloned.1.call-start = ((), (), s32[]{:S(2)}) async-start(), calls=%async_computation.27 | async-start | bytes 48234496 | tf_op jit(solution)/shard_map/psum | solution.py:316
  (78 other events, 645.4 us)
Sparse Core Ops, SparseCore 0:
  9.6 152.3 all-gather.11
  163.5 147.8 all-gather.17
  313.0 148.0 all-gather.15
  463.0 44.0 all-gather.13
  509.2 44.6 all-gather.19
  555.3 148.3 all-gather.21
  705.2 355.0 all-gather.23
  1061.9 355.3 all-gather.25
  1418.9 355.3 all-gather.27
  1932.7 42.4 reduce-scatter.27
  1978.1 43.1 reduce-scatter.29
  2024.2 143.7 reduce-scatter.13
  2170.3 145.1 reduce-scatter.19
  2318.4 145.1 reduce-scatter.15
  2466.4 145.1 reduce-scatter.17
  2613.8 347.9 reduce-scatter.21
  2964.1 348.6 reduce-scatter.23
  3315.0 348.6 reduce-scatter.25
  3669.7 301.8 all-reduce.10
where the time goes:
time: 4020 us; the launch traced here: 4010 us
  waiting for transfers between devices  3530 us (88%)
  matrix products  211 us (5%)
  local copies, waits for them, and re-layouts  118 us (3%)
  blocking collectives  74.6 us (2%)
  other arithmetic  50.8 us (1%)
    all_gather x1, waiting for transfers between devices, local(): lax.all_gather(w_gate, 'group', axis=1, tiled=True)  352 us
    reduce_scatter x1, waiting for transfers between devices, local(): lax.psum_scatter(inner_rows(normed_two, grad_up).astype(jnp.bfloat16), 'g...  351 us
    reduce_scatter x1, waiting for transfers between devices, local(): lax.psum_scatter(inner_rows(hidden_low, grad_low).astype(jnp.bfloat16), '...  351 us
    reduce_scatter x1, waiting for transfers between devices, local(): lax.psum_scatter(inner_rows(normed_two, grad_gate).astype(jnp.bfloat16),...  350 us
    all_gather x1, waiting for transfers between devices, local(): lax.all_gather(w_ffn_out, 'group', axis=0, tiled=True)  345 us
    all_gather x1, waiting for transfers between devices, local(): lax.all_gather(w_up, 'group', axis=1, tiled=True)  345 us
    psum x1, waiting for transfers between devices, local(): lax.psum(query_part.astype(jnp.bfloat16), 'replica').astype(jnp.float32)  245 us
    reduce_scatter x1, waiting for transfers between devices, local(): lax.psum_scatter(key_grad.astype(jnp.bfloat16), 'group', scatter_dimensio...  148 us
  transfers between devices with their start and end apart: 19, of which 19 were waited for; matrix products, arithmetic and copies ran while one was open for 4% of the time, Pallas kernels for 0%

commit v1 on v0

--- a/solution.py
+++ b/solution.py
@@ -7,6 +7,27 @@
 negative = -1000000000.0
 head_block = 8
 highest = lax.Precision.HIGHEST
+
+
+def laid_out(pieces, dim):
+    dims = list(pieces.shape[1:])
+    dims[dim] *= pieces.shape[0]
+    return jnp.moveaxis(pieces, 0, dim).reshape(dims)
+
+
+def doubled(value, axis):
+    length, here = (lax.axis_size(axis), lax.axis_index(axis))
+    blocks, apart = (value[None], 1)
+    while apart < length:
+        other = lax.ppermute(blocks, axis, [(i, i ^ apart) for i in range(length)])
+        low = here & apart == 0
+        blocks = jnp.concatenate([jnp.where(low, blocks, other), jnp.where(low, other, blocks)])
+        apart *= 2
+    return blocks
+
+
+def gather_by_bits(x, axis, dim):
+    return laid_out(doubled(x, axis), dim)
 
 
 def rms_scale(values, gain):
@@ -168,7 +189,7 @@
         lax.all_gather(w_query, "group", axis=1, tiled=True),
         lax.all_gather(w_key, "group", axis=1, tiled=True),
         lax.all_gather(w_value, "group", axis=1, tiled=True),
-        lax.all_gather(w_attn_out, "group", axis=0, tiled=True),
+        gather_by_bits(w_attn_out, "group", 0),
         lax.all_gather(bias_table, "group", axis=1, tiled=True),
     )
     gain_first = gain_one.astype(jnp.float32)

time: 4020 us -> 4150 us (1.032)
  blocking collectives: 74.6 us -> 376 us
  waiting for transfers between devices: 3530 us -> 3340 us
    all_gather x1, blocking collectives: 15.4 us -> 302 us  [local(): lax.all_gather(norm2_gain, 'group', axis=0, tiled=True)]
    all_gather x1, waiting for transfers between devices: 352 us -> 183 us  [local(): lax.all_gather(w_gate, 'group', axis=1, tiled=True)]
    ppermute x0 -> x2, waiting for transfers between devices: none -> 160 us  [doubled(): other = lax.ppermute(blocks, axis, [(i, i ^ apart) for i in range(length)])]
    all_gather x1, waiting for transfers between devices: 111 us -> 0.01 us  [local(): lax.all_gather(w_query, 'group', axis=1, tiled=True)]
    all_gather x1, waiting for transfers between devices: 42.8 us -> 0.01 us  [local(): lax.all_gather(key_low, 'group', axis=0, tiled=True)]
  transfers between devices with their start and end apart: 19 -> 21, of which waited for: 19 -> 17; matrix products, arithmetic and copies ran while one was open for 4% -> 6% of each run, Pallas kernels for 0% -> 0%
where the time goes in v1:
time: 4150 us; the launch traced here: 4140 us
  waiting for transfers between devices  3340 us (80%)
  blocking collectives  376 us (9%)
  matrix products  213 us (5%)
  local copies, waits for them, and re-layouts  118 us (3%)
  other arithmetic  67.7 us (2%)
    reduce_scatter x1, waiting for transfers between devices, local(): lax.psum_scatter(inner_rows(normed_two, grad_up).astype(jnp.bfloat16), 'g...  351 us
    reduce_scatter x1, waiting for transfers between devices, local(): lax.psum_scatter(inner_rows(hidden_low, grad_low).astype(jnp.bfloat16), '...  351 us
    reduce_scatter x1, waiting for transfers between devices, local(): lax.psum_scatter(inner_rows(normed_two, grad_gate).astype(jnp.bfloat16),...  350 us
    all_gather x1, waiting for transfers between devices, local(): lax.all_gather(w_ffn_out, 'group', axis=0, tiled=True)  345 us
    all_gather x1, waiting for transfers between devices, local(): lax.all_gather(w_up, 'group', axis=1, tiled=True)  345 us
    all_gather x1, blocking collectives, local(): lax.all_gather(norm2_gain, 'group', axis=0, tiled=True)  302 us
    psum x1, waiting for transfers between devices, local(): lax.psum(query_part.astype(jnp.bfloat16), 'replica').astype(jnp.float32)  245 us
    all_gather x1, waiting for transfers between devices, local(): lax.all_gather(w_gate, 'group', axis=1, tiled=True)  183 us
  transfers between devices with their start and end apart: 21, of which 17 were waited for; matrix products, arithmetic and copies ran while one was open for 6% of the time, Pallas kernels for 0%

profile of v1, /device:TPU:0, one launch (start us, length us, event | category | flops | bytes accessed | tf_op | source)
XLA Modules:
  0.0 4135.8 jit_solution(6860282864198943273)
XLA Ops:
  9.5 13.5 all-gather
  23.3 138.7 %all-gather.12.cloned.1.call-done = bf16[2048,2048]{1,0:T(8,128)(2,1)} async-done(((bf16[2048,512]{1,0:T(8,128)(2,1)}), bf16[2048,2048]{1,0:T(8,128)(2,1)}) %all-gather.12.cloned.1.call-update) | async-done | bytes 8388624 | tf_op jit(solution)/shard_map/all_gather | solution.py:191
  167.5 143.9 %all-gather.18.cloned.1.call-done = bf16[2048,2048]{1,0:T(8,128)(2,1)} async-done(((bf16[2048,512]{1,0:T(8,128)(2,1)}), bf16[2048,2048]{1,0:T(8,128)(2,1)}) %all-gather.18.cloned.1.call-update) | async-done | bytes 8388624 | tf_op jit(solution)/shard_map/all_gather | solution.py:190
  320.1 160.0 %collective-permute-done = bf16[1,512,2048]{2,1,0:T(8,128)(2,1)} collective-permute-done((bf16[1,512,2048]{2,1,0:T(8,128)(2,1)S(1)}, bf16[1,512,2048]{2,1,0:T(8,128)(2,1)}, u32[]{:S(2)}, u32[]{:S(2)}) %collective-permute-start) | collective-permute-done | bytes 2097184 | tf_op jit(solution)/shard_map/ppermute | solution.py:22
  485.6 301.5 %all-gather.1 = bf16[4,1,512]{2,1,0:T(2,128)(2,1)S(1)} all-gather(bf16[1,1,512]{2,1,0:T(2,128)(2,1)S(1)} %reshape.203), channel_id=1, replica_groups=mesh['replica'=8,'group'=4] {'group'}, dimensions={0}, use_global_device_ids=true | all-gather | bytes 5120 | tf_op jit(solution)/shard_map/all_gather | solution.py:188
  787.8 29.2 all_gather.49
  845.1 45.2 %while.32 = (s32[]{:T(128)}, bf16[4,128,8,64]{1,3,2,0:T(8,128)(2,1)}, f32[4,8,128]{2,1,0:T(8,128)S(1)}, bf16[4,512,8,64]{1,3,2,0:T(8,128)(2,1)}, bf16[4,128,8,64...) while((s32[]{:T(128)}, ...), condition=%wide.region_4.5_spmd.clone, body=%wide.region_1.4_spmd.clone.sunk | while | flops 138411520 | bytes 35106080 | solution.py:111
  895.5 183.0 %all-gather.22.cloned.1.call-done = bf16[2048,5120]{1,0:T(8,128)(2,1)} async-done(((bf16[2048,1280]{1,0:T(8,128)(2,1)}), bf16[2048,5120]{1,0:T(8,128)(2,1)}) %all-gather.22.cloned.1.call-update) | async-done | bytes 20971536 | tf_op jit(solution)/shard_map/all_gather | solution.py:224
  1090.4 344.9 %all-gather.24.cloned.1.call-done = bf16[2048,5120]{1,0:T(8,128)(2,1)} async-done(((bf16[2048,1280]{1,0:T(8,128)(2,1)}), bf16[2048,5120]{1,0:T(8,128)(2,1)}) %all-gather.24.cloned.1.call-update) | async-done | bytes 20971536 | tf_op jit(solution)/shard_map/all_gather | solution.py:225
  1447.0 345.3 %all-gather.26.cloned.1.call-done = bf16[5120,2048]{1,0:T(8,128)(2,1)} async-done(((bf16[1280,2048]{1,0:T(8,128)(2,1)}), bf16[5120,2048]{1,0:T(8,128)(2,1)}) %all-gather.26.cloned.1.call-update) | async-done | bytes 20971536 | tf_op jit(solution)/shard_map/all_gather | solution.py:226
  1792.3 14.6 multiply_convert_fusion.1
  1831.6 110.6 %all-gather.28.cloned.1.call-done = bf16[2048,2048]{1,0:T(8,128)(2,1)} async-done(((bf16[512,2048]{1,0:T(8,128)(2,1)}), bf16[2048,2048]{1,0:T(8,128)(2,1)}) %all-gather.28.cloned.1.call-update) | async-done | bytes 8388624 | tf_op jit(solution)/shard_map/all_gather | solution.py:272
  1950.4 106.6 %while.33 = (s32[]{:T(128)}, bf16[4,128,8,64]{1,3,2,0:T(8,128)(2,1)}, bf16[4,512,8,64]{1,3,2,0:T(8,128)(2,1)}, bf16[4,512,8,64]{1,3,2,0:T(8,128)(2,1)}, f32[4,8,...) while((s32[]{:T(128)}, ...), condition=%wide.region_10.11_spmd.clone, body=%wide.region_7.10_spmd.clone.sunk | while | flops 341570048 | bytes 102152648 | solution.py:153
  2077.6 25.8 reduce-scatter.28.cloned.1.call-done
  2110.3 39.2 reduce-scatter.30.cloned.1.call-done
  2191.6 104.5 %reduce-scatter.14.cloned.1.call-done = bf16[2048,512]{1,0:T(8,128)(2,1)} async-done(((bf16[2048,2048]{1,0:T(8,128)(2,1)}), bf16[2048,512]{1,0:T(8,128)(2,1)}) %reduce-scatter.14.cloned.1.call-update) | async-done | bytes 2097168 | tf_op jit(solution)/shard_map/reduce_scatter | solution.py:319
  2296.1 147.6 %reduce-scatter.20.cloned.1.call-done = bf16[512,2048]{1,0:T(8,128)(2,1)} async-done(((bf16[2048,2048]{1,0:T(8,128)(2,1)}), bf16[512,2048]{1,0:T(8,128)(2,1)}) %reduce-scatter.20.cloned.1.call-update) | async-done | bytes 2097168 | tf_op jit(solution)/shard_map/reduce_scatter | solution.py:328
  2443.7 148.0 %reduce-scatter.16.cloned.1.call-done = bf16[2048,512]{1,0:T(8,128)(2,1)} async-done(((bf16[2048,2048]{1,0:T(8,128)(2,1)}), bf16[2048,512]{1,0:T(8,128)(2,1)}) %reduce-scatter.16.cloned.1.call-update) | async-done | bytes 2097168 | tf_op jit(solution)/shard_map/reduce_scatter | solution.py:322
  2591.7 148.0 %reduce-scatter.18.cloned.1.call-done = bf16[2048,512]{1,0:T(8,128)(2,1)} async-done(((bf16[2048,2048]{1,0:T(8,128)(2,1)}), bf16[2048,512]{1,0:T(8,128)(2,1)}) %reduce-scatter.18.cloned.1.call-update) | async-done | bytes 2097168 | tf_op jit(solution)/shard_map/reduce_scatter | solution.py:325
  2739.8 350.2 %reduce-scatter.22.cloned.1.call-done = bf16[2048,1280]{1,0:T(8,128)(2,1)} async-done(((bf16[2048,5120]{1,0:T(8,128)(2,1)}), bf16[2048,1280]{1,0:T(8,128)(2,1)}) %reduce-scatter.22.cloned.1.call-update) | async-done | bytes 5242896 | tf_op jit(solution)/shard_map/reduce_scatter | solution.py:245
  3089.9 351.0 %reduce-scatter.24.cloned.1.call-done = bf16[2048,1280]{1,0:T(8,128)(2,1)} async-done(((bf16[2048,5120]{1,0:T(8,128)(2,1)}), bf16[2048,1280]{1,0:T(8,128)(2,1)}) %reduce-scatter.24.cloned.1.call-update) | async-done | bytes 5242896 | tf_op jit(solution)/shard_map/reduce_scatter | solution.py:251
  3440.9 350.9 %reduce-scatter.26.cloned.1.call-done = bf16[1280,2048]{1,0:T(8,128)(2,1)} async-done(((bf16[5120,2048]{1,0:T(8,128)(2,1)}), bf16[1280,2048]{1,0:T(8,128)(2,1)}) %reduce-scatter.26.cloned.1.call-update) | async-done | bytes 5242896 | tf_op jit(solution)/shard_map/reduce_scatter | solution.py:257
  3819.4 18.9 all-reduce.8
  3854.5 245.3 %all-reduce.11.cloned.1.call-done = (bf16[2048,512]{1,0:T(8,128)(2,1)}, bf16[2048,512]{1,0:T(8,128)(2,1)}, bf16[2048,512]{1,0:T(8,128)(2,1)}, bf16[512,2048]{1,0...) async-done(((bf16[2048,512]{1,0:T(8,128)(2,1)}, bf16[2048,512]{1,0:T(8,128)(2,1)}, bf16[2048,512]{1,0:T(8,128)(2,1)}, ...) | async-done | bytes 24117264 | tf_op jit(solution)/shard_map/psum | solution.py:337
  (393 shorter events, 402.7 us)
Async XLA Ops:
  7.2 154.8 %all-gather.12.cloned.1.call-start = ((), (), s32[]{:S(2)}) async-start(), calls=%async_computation.9 | async-start | bytes 10485760 | tf_op jit(solution)/shard_map/all_gather | solution.py:191
  7.9 303.5 %all-gather.18.cloned.1.call-start = ((), (), s32[]{:S(2)}) async-start(), calls=%async_computation.12 | async-start | bytes 10485760 | tf_op jit(solution)/shard_map/all_gather | solution.py:190
  8.7 821.9 %all-gather.16.cloned.1.call-start = ((), (), s32[]{:S(2)}) async-start(), calls=%async_computation.11 | async-start | bytes 10485760 | tf_op jit(solution)/shard_map/all_gather | solution.py:189
  9.4 826.9 %all-gather.14.cloned.1.call-start = ((), (), s32[]{:S(2)}) async-start(), calls=%async_computation.10 | async-start | bytes 2621440 | tf_op jit(solution)/shard_map/all_gather | solution.py:209
  23.1 807.5 %copy-start.19 = (f32[4,1,512]{2,1,0:T(1,128)}, f32[4,1,512]{2,1,0:T(1,128)S(1)}, u32[]{:S(2)}) copy-start(f32[4,1,512]{2,1,0:T(1,128)S(1)} %convert_element_type.285) | copy-start | bytes 24580
  23.3 807.3 %copy-start.33 = (f32[128]{0:T(128)}, f32[128]{0:T(128)S(1)}, u32[]{:S(2)}) copy-start(f32[128]{0:T(128)S(1)} %fusion.81) | copy-start | bytes 1540
  167.5 672.7 %all-gather.20.cloned.1.call-start = ((), (), s32[]{:S(2)}) async-start(), calls=%async_computation.13 | async-start | bytes 2621440 | tf_op jit(solution)/shard_map/all_gather | solution.py:208
  316.9 761.7 %all-gather.22.cloned.1.call-start = ((), (), s32[]{:S(2)}) async-start(), calls=%async_computation.14 | async-start | bytes 26214400 | tf_op jit(solution)/shard_map/all_gather | solution.py:224
  317.5 1117.8 %all-gather.24.cloned.1.call-start = ((), (), s32[]{:S(2)}) async-start(), calls=%async_computation.15 | async-start | bytes 26214400 | tf_op jit(solution)/shard_map/all_gather | solution.py:225
  318.2 1474.1 %all-gather.26.cloned.1.call-start = ((), (), s32[]{:S(2)}) async-start(), calls=%async_computation.16 | async-start | bytes 26214400 | tf_op jit(solution)/shard_map/all_gather | solution.py:226
  319.0 1623.2 %all-gather.28.cloned.1.call-start = ((), (), s32[]{:S(2)}) async-start(), calls=%async_computation.17 | async-start | bytes 10485760 | tf_op jit(solution)/shard_map/all_gather | solution.py:272
  320.1 160.0 %collective-permute-start = (bf16[1,512,2048]{2,1,0:T(8,128)(2,1)S(1)}, bf16[1,512,2048]{2,1,0:T(8,128)(2,1)}, u32[]{:S(2)}, u32[]{:S(2)}) collective-permute-start(bf16[1,512,2048]{2,1,0:T(8,128)(2,1)S(1)} %bitcast.279), channel_id=1, source_target_pairs={{0,1},{1,0},{2,3},{3,2},{4,5},{5,4},{6,7},{7,6},{8,9},{9,8},{10,11... | collective-permute-start | bytes 6291464 | tf_op jit(solution)/shard_map/ppermute | solution.py:22
  485.4 332.0 %collective-permute-start.1 = (bf16[2,512,2048]{2,1,0:T(8,128)(2,1)}, bf16[2,512,2048]{2,1,0:T(8,128)(2,1)}, u32[]{:S(2)}, u32[]{:S(2)}) collective-permute-start(bf16[2,512,2048]{2,1,0:T(8,128)(2,1)} %pad_maximum_fusion.1), channel_id=1, source_target_pairs={{0,2},{1,3},{2,0},{3,1},{4,6},{5,7},{6,4},{7,5},{8,10},{9,11},{10,... | collective-permute-start | bytes 12582920 | tf_op jit(solution)/shard_map/ppermute | solution.py:22
  485.4 1617.9 %reduce-scatter.28.cloned.1.call-start = ((), (), s32[]{:S(2)}) async-start(), calls=%async_computation.25 | async-start | bytes 2621440
  895.3 935.9 %copy-start.3 = (f32[128,2048]{1,0:T(8,128)}, f32[128,2048]{1,0:T(8,128)S(1)}, u32[]{:S(2)}) copy-start(f32[128,2048]{1,0:T(8,128)S(1)} %get-tuple-element.328) | copy-start | bytes 3145732
  2061.1 88.5 %reduce-scatter.30.cloned.1.call-start = ((), (), s32[]{:S(2)}) async-start(), calls=%async_computation.26 | async-start | bytes 2621440
  2063.6 232.6 %reduce-scatter.14.cloned.1.call-start = ((), (), s32[]{:S(2)}) async-start(), calls=%async_computation.18 | async-start | bytes 10485760 | tf_op jit(solution)/shard_map/reduce_scatter | solution.py:319
  2070.6 373.2 %reduce-scatter.20.cloned.1.call-start = ((), (), s32[]{:S(2)}) async-start(), calls=%async_computation.21 | async-start | bytes 10485760 | tf_op jit(solution)/shard_map/reduce_scatter | solution.py:328
  2077.5 514.2 %reduce-scatter.16.cloned.1.call-start = ((), (), s32[]{:S(2)}) async-start(), calls=%async_computation.19 | async-start | bytes 10485760 | tf_op jit(solution)/shard_map/reduce_scatter | solution.py:322
  2110.2 629.5 %reduce-scatter.18.cloned.1.call-start = ((), (), s32[]{:S(2)}) async-start(), calls=%async_computation.20 | async-start | bytes 10485760 | tf_op jit(solution)/shard_map/reduce_scatter | solution.py:325
  2156.4 933.5 %reduce-scatter.22.cloned.1.call-start = ((), (), s32[]{:S(2)}) async-start(), calls=%async_computation.22 | async-start | bytes 26214400 | tf_op jit(solution)/shard_map/reduce_scatter | solution.py:245
  2168.4 1272.5 %reduce-scatter.24.cloned.1.call-start = ((), (), s32[]{:S(2)}) async-start(), calls=%async_computation.23 | async-start | bytes 26214400 | tf_op jit(solution)/shard_map/reduce_scatter | solution.py:251
  2179.9 1612.0 %reduce-scatter.26.cloned.1.call-start = ((), (), s32[]{:S(2)}) async-start(), calls=%async_computation.24 | async-start | bytes 26214400 | tf_op jit(solution)/shard_map/reduce_scatter | solution.py:257
  2191.3 1908.4 %all-reduce.11.cloned.1.call-start = ((), (), s32[]{:S(2)}) async-start(), calls=%async_computation.27 | async-start | bytes 48234496 | tf_op jit(solution)/shard_map/psum | solution.py:337
  (81 other events, 2470.2 us)
Sparse Core Ops, SparseCore 0:
  9.6 152.3 all-gather.11
  163.5 147.8 all-gather.17
  313.0 202.9 all-gather.15
  518.0 125.3 all-gather.13
  645.3 63.0 all-gather.19
  709.9 368.6 all-gather.21
  1080.1 355.1 all-gather.23
  1436.9 355.3 all-gather.25
  1793.9 148.1 all-gather.27
  2061.2 42.0 reduce-scatter.27
  2106.3 43.1 reduce-scatter.29
  2152.3 143.7 reduce-scatter.13
  2298.5 145.1 reduce-scatter.19
  2446.5 145.1 reduce-scatter.15
  2594.5 145.1 reduce-scatter.17
  2742.0 347.9 reduce-scatter.21
  3092.3 348.6 reduce-scatter.23
  3443.2 348.6 reduce-scatter.25
  3797.8 301.8 all-reduce.10
